TPU v7x, 256 devices: a whole 4x4x8 slice. The times are simulated.
256 devices in a mesh: layer: 2 (over x_lo), row: 32 (over z, y), col: 4 (over x_hi, core).
Axes of the slice: x: 4 (x_hi: 2, x_lo: 2; x = x_hi * 2 + x_lo), y: 4, z: 8, core: 2. Of those that a mesh axis runs over, the one named last changes fastest.
Arguments:
- rhs_root: float32 [16384, 128], P('col'), may hold values from -6 to 6
- rhs_child: float32 [2, 8192, 128], P('layer', 'col'), may hold values from -6 to 6
- rhs_leaf: float32 [4, 4096, 128], P('layer', 'col'), may hold values from -6 to 6
- root_inv: bfloat16 [16384, 16384], P('row', 'col'), may hold values from -0.046875 to 0.046875
- child_inv: bfloat16 [2, 8192, 8192], P('layer', 'row', 'col'), may hold values from -0.0625 to 0.0625
- leaf_inv: bfloat16 [4, 4096, 4096], P('layer', 'row', 'col'), may hold values from -0.09375 to 0.09375
- leaf_to_child: bfloat16 [4, 8192, 4096], P('layer', 'col', 'row'), may hold values from -0.0625 to 0.0625
- leaf_to_root: bfloat16 [4, 16384, 4096], P('layer', 'col', 'row'), may hold values from -0.03125 to 0.03125
- child_to_root: bfloat16 [2, 16384, 8192], P('layer', 'col', 'row'), may hold values from -0.03125 to 0.03125
Outputs:
- x_root: float32 [16384, 128], P('col')
- x_child: float32 [2, 8192, 128], P('layer', 'col')
- x_leaf: float32 [4, 4096, 128], P('layer', 'col')
- y_root: float32 [16384, 128], P('row')
All inputs are finite; a program needn't handle non-finite values.
Results may differ from a plain program's by a relative error of at most 0.008.
Values sent between devices are 32-bit elements; how exact they have to be, the bound alone decides.
No kernel may reach another device: no remote copies, remote signals or barrier semaphores. Data moves between devices by JAX's collectives and lax.ppermute only.
A program may use at most 64 MiB of HBM per device.

v0:
```python
import jax
import jax.numpy as jnp
from jax import lax
from jax.sharding import PartitionSpec as P


def col_sum(values):
    return lax.psum(values, "col")


def row_sum(values):
    return lax.psum(values, "row")


def root_total(values):
    return lax.psum(values, ("layer", "row"))


def half16(values):
    return values.astype(jnp.bfloat16)


def on_device(
    rhs_root,
    rhs_child,
    rhs_leaf,
    root_inv,
    child_inv,
    leaf_inv,
    leaf_to_child,
    leaf_to_root,
    child_to_root,
):
    f32 = jnp.float32
    y_leaf = col_sum(
        jnp.einsum("gij,gjs->gis", leaf_inv, half16(rhs_leaf), preferred_element_type=f32)
    )
    leaf_bf = half16(y_leaf)
    leaf_update = jnp.einsum("gij,gjs->is", leaf_to_root, leaf_bf, preferred_element_type=f32)
    r_child = rhs_child[0] - row_sum(
        jnp.einsum("gij,gjs->is", leaf_to_child, leaf_bf, preferred_element_type=f32)
    )
    y_child = col_sum(jnp.dot(child_inv[0], half16(r_child), preferred_element_type=f32))
    child_update = jnp.dot(child_to_root[0], half16(y_child), preferred_element_type=f32)
    r_root = rhs_root - root_total(child_update + leaf_update)
    y_root = col_sum(jnp.dot(root_inv, half16(r_root), preferred_element_type=f32))
    x_root = row_sum(jnp.einsum("ij,is->js", root_inv, half16(y_root), preferred_element_type=f32))
    root_bf = half16(x_root)
    back_child = y_child - col_sum(
        jnp.einsum("ij,is->js", child_to_root[0], root_bf, preferred_element_type=f32)
    )
    x_child = row_sum(
        jnp.einsum("ij,is->js", child_inv[0], half16(back_child), preferred_element_type=f32)
    )
    terms = jnp.einsum("gij,is->gjs", leaf_to_child, half16(x_child), preferred_element_type=f32)
    terms = terms + jnp.einsum("gij,is->gjs", leaf_to_root, root_bf, preferred_element_type=f32)
    back_leaf = y_leaf - col_sum(terms)
    x_leaf = row_sum(
        jnp.einsum("gij,gis->gjs", leaf_inv, half16(back_leaf), preferred_element_type=f32)
    )
    return (x_root, x_child[None], x_leaf, y_root)


def solution(mesh):
    in_specs = (
        P("col", None),
        P("layer", "col", None),
        P("layer", "col", None),
        P("row", "col"),
        P("layer", "row", "col"),
        P("layer", "row", "col"),
        P("layer", "col", "row"),
        P("layer", "col", "row"),
        P("layer", "col", "row"),
    )
    out_specs = (P("col", None), P("layer", "col", None), P("layer", "col", None), P("row", None))
    return jax.shard_map(
        on_device, mesh=mesh, in_specs=in_specs, out_specs=out_specs, check_vma=False
    )
```

profile of v0, /device:TPU:2, one launch (start us, length us, event | category | flops | bytes accessed | tf_op | source)
XLA Modules:
  0.0 1495.1 jit_solution(6463682180785090896)
XLA Ops:
  7.2 2.5 fusion.18
  9.7 0.0 all-reduce.13.cloned.1.call-start
  9.8 48.8 %all-reduce.11.cloned.1.call-done = f32[2,128,128]{2,1,0:T(8,128)} async-done(((f32[2,128,128]{2,1,0:T(8,128)}), f32[2,128,128]{2,1,0:T(8,128)}) %all-reduce.11.cloned.1.call-update) | async-done | bytes 131088 | tf_op jit(solution)/shard_map/psum | solution.py:8
  58.5 2.6 convolution_bitcast_fusion.2
  61.2 0.0 all-reduce.15.cloned.1.call-start
  61.2 152.3 %all-reduce.13.cloned.1.call-done = f32[2048,128]{1,0:T(8,128)} async-done(((f32[2048,128]{1,0:T(8,128)}), f32[2048,128]{1,0:T(8,128)}) %all-reduce.13.cloned.1.call-update) | async-done | bytes 1048592 | tf_op jit(solution)/shard_map/psum | solution.py:12
  213.5 2.7 convolution_bitcast_fusion.6
  216.3 0.0 all-reduce.17.cloned.1.call-start
  216.3 3.6 convolution_bitcast_fusion
  219.9 38.4 %all-reduce.15.cloned.1.call-done = f32[256,128]{0,1:T(8,128)} async-done(((f32[256,128]{0,1:T(8,128)}), f32[256,128]{0,1:T(8,128)}) %all-reduce.15.cloned.1.call-update) | async-done | bytes 131088 | tf_op jit(solution)/shard_map/psum | solution.py:8
  258.3 3.7 fusion
  262.1 612.7 %all-reduce.17.cloned.1.call-done = f32[4096,128]{1,0:T(8,128)} async-done(((f32[4096,128]{1,0:T(8,128)}), f32[4096,128]{1,0:T(8,128)}) %all-reduce.17.cloned.1.call-update) | async-done | bytes 2097168 | tf_op jit(solution)/shard_map/psum | solution.py:16
  874.8 5.7 convolution_bitcast_fusion.5
  880.6 0.0 all-reduce.21.cloned.1.call-start
  880.6 43.7 %all-reduce.19.cloned.1.call-done = f32[512,128]{0,1:T(8,128)} async-done(((f32[512,128]{0,1:T(8,128)}), f32[512,128]{0,1:T(8,128)}) %all-reduce.19.cloned.1.call-update) | async-done | bytes 262160 | tf_op jit(solution)/shard_map/psum | solution.py:8
  924.4 4.3 convolution_bitcast_fusion.1
  928.7 0.0 all-reduce.23.cloned.1.call-start
  928.8 154.9 %all-reduce.21.cloned.1.call-done = f32[4096,128]{0,1:T(8,128)} async-done(((f32[4096,128]{0,1:T(8,128)}), f32[4096,128]{0,1:T(8,128)}) %all-reduce.21.cloned.1.call-update) | async-done | bytes 2097168 | tf_op jit(solution)/shard_map/psum | solution.py:12
  1083.7 2.7 fusion.4
  1086.5 42.2 %all-reduce.23.cloned.1.call-done = f32[256,128]{0,1:T(8,128)} async-done(((f32[256,128]{0,1:T(8,128)}), f32[256,128]{0,1:T(8,128)}) %all-reduce.23.cloned.1.call-update) | async-done | bytes 131088 | tf_op jit(solution)/shard_map/psum | solution.py:8
  1128.7 2.2 convolution_bitcast_fusion.3
  1130.9 0.0 all-reduce.27.cloned.1.call-start
  1131.0 152.7 %all-reduce.25.cloned.1.call-done = f32[2048,128]{0,1:T(8,128)} async-done(((f32[2048,128]{0,1:T(8,128)}), f32[2048,128]{0,1:T(8,128)}) %all-reduce.25.cloned.1.call-update) | async-done | bytes 1048592 | tf_op jit(solution)/shard_map/psum | solution.py:12
  1283.7 2.2 fusion.13
  1285.9 3.1 fusion.7
  1289.2 41.6 %all-reduce.27.cloned.1.call-done = f32[2,128,128]{2,1,0:T(8,128)} async-done(((f32[2,128,128]{2,1,0:T(8,128)}), f32[2,128,128]{2,1,0:T(8,128)}) %all-reduce.27.cloned.1.call-update) | async-done | bytes 131088 | tf_op jit(solution)/shard_map/psum | solution.py:8
  1330.8 2.2 convolution_bitcast_fusion.4
  1333.1 0.8 copy.17
  1333.9 3.0 copy.14
  1336.9 1.3 copy.15
  1338.2 147.5 %all-reduce.29.cloned.1.call-done = f32[2,1024,128]{1,2,0:T(8,128)} async-done(((f32[2,1024,128]{1,2,0:T(8,128)}), f32[2,1024,128]{1,2,0:T(8,128)}) %all-reduce.29.cloned.1.call-update) | async-done | bytes 1048592 | tf_op jit(solution)/shard_map/psum | solution.py:12
  1485.7 2.5 copy.16
  (30 shorter events, 0.4 us)
Async XLA Ops:
  7.2 251.2 %copy-start = (bf16[1,4096,256]{2,1,0:T(8,128)(2,1)S(1)}, bf16[1,4096,256]{2,1,0:T(8,128)(2,1)}, u32[]{:S(2)}) copy-start(bf16[1,4096,256]{2,1,0:T(8,128)(2,1)} %param.17) | copy-start | bytes 6291460
  7.2 51.4 %all-reduce.11.cloned.1.call-start = ((), (), s32[]{:S(2)}) async-start(), calls=%async_computation | async-start | bytes 262144 | tf_op jit(solution)/shard_map/psum | solution.py:8
  9.7 203.8 %copy-start.2 = (bf16[1,256,2048]{2,1,0:T(8,128)(2,1)S(1)}, bf16[1,256,2048]{2,1,0:T(8,128)(2,1)}, u32[]{:S(2)}) copy-start(bf16[1,256,2048]{2,1,0:T(8,128)(2,1)} %param.13) | copy-start | bytes 3145732
  9.7 203.8 %all-reduce.13.cloned.1.call-start = ((), (), s32[]{:S(2)}) async-start(), calls=%async_computation.1 | async-start | bytes 2097152 | tf_op jit(solution)/shard_map/psum | solution.py:12
  61.2 155.1 %copy-start.5 = (f32[2,128,128]{2,1,0:T(8,128)S(1)}, f32[2,128,128]{2,1,0:T(8,128)}, u32[]{:S(2)}) copy-start(f32[2,128,128]{2,1,0:T(8,128)} %all-reduce.11.cloned.1.call-done) | copy-start | bytes 393220
  61.2 197.1 %all-reduce.15.cloned.1.call-start = ((), (), s32[]{:S(2)}) async-start(), calls=%async_computation.2 | async-start | bytes 262144 | tf_op jit(solution)/shard_map/psum | solution.py:8
  216.3 658.6 %all-reduce.17.cloned.1.call-start = ((), (), s32[]{:S(2)}) async-start(), calls=%async_computation.3 | async-start | bytes 4194304 | tf_op jit(solution)/shard_map/psum | solution.py:16
  262.0 662.3 %all-reduce.19.cloned.1.call-start = ((), (), s32[]{:S(2)}) async-start(), calls=%async_computation.4 | async-start | bytes 524288 | tf_op jit(solution)/shard_map/psum | solution.py:8
  880.6 203.1 %all-reduce.21.cloned.1.call-start = ((), (), s32[]{:S(2)}) async-start(), calls=%async_computation.5 | async-start | bytes 4194304 | tf_op jit(solution)/shard_map/psum | solution.py:12
  928.7 200.0 %copy-start.7 = (f32[256,128]{0,1:T(8,128)S(1)}, f32[256,128]{0,1:T(8,128)}, u32[]{:S(2)}) copy-start(f32[256,128]{0,1:T(8,128)} %all-reduce.15.cloned.1.call-done) | copy-start | bytes 393220
  928.7 200.0 %all-reduce.23.cloned.1.call-start = ((), (), s32[]{:S(2)}) async-start(), calls=%async_computation.6 | async-start | bytes 262144 | tf_op jit(solution)/shard_map/psum | solution.py:8
  1086.4 197.3 %all-reduce.25.cloned.1.call-start = ((), (), s32[]{:S(2)}) async-start(), calls=%async_computation.7 | async-start | bytes 2097152 | tf_op jit(solution)/shard_map/psum | solution.py:12
  1130.9 199.9 %all-reduce.27.cloned.1.call-start = ((), (), s32[]{:S(2)}) async-start(), calls=%async_computation.8 | async-start | bytes 262144 | tf_op jit(solution)/shard_map/psum | solution.py:8
  1283.7 2.2 copy-start.1
  1285.9 44.9 %copy-start.4 = (bf16[2,128,1024]{2,1,0:T(8,128)(2,1)S(1)}, bf16[2,128,1024]{2,1,0:T(8,128)(2,1)}, u32[]{:S(2)}) copy-start(bf16[2,128,1024]{2,1,0:T(8,128)(2,1)} %param.14) | copy-start | bytes 1572868
  1289.1 44.0 %copy-start.6 = (f32[512,128]{0,1:T(8,128)S(1)}, f32[512,128]{0,1:T(8,128)}, u32[]{:S(2)}) copy-start(f32[512,128]{0,1:T(8,128)} %all-reduce.19.cloned.1.call-done) | copy-start | bytes 786436
  1289.1 196.6 %all-reduce.29.cloned.1.call-start = ((), (), s32[]{:S(2)}) async-start(), calls=%async_computation.9 | async-start | bytes 2097152 | tf_op jit(solution)/shard_map/psum | solution.py:12
  1333.9 3.0 copy-start.3
Sparse Core Ops, SparseCore 0:
  11.2 47.3 all-reduce.10
  62.6 150.9 all-reduce.12
  216.7 41.5 all-reduce.14
  262.2 612.6 all-reduce.16
  880.7 43.6 all-reduce.18
  928.8 154.8 all-reduce.20
  1086.9 41.7 all-reduce.22
  1132.7 150.9 all-reduce.24
  1289.2 41.5 all-reduce.26
  1334.7 150.9 all-reduce.28
where the time goes:
time: 1500 us
  waiting for transfers between devices  1440 us (96%)
  matrix products  37.6 us (3%)
    psum x1, waiting for transfers between devices, root_total(): return lax.psum(values, ('layer', 'row'))  613 us
    psum x4, waiting for transfers between devices, row_sum(): return lax.psum(values, 'row')  607 us
    psum x5, waiting for transfers between devices, col_sum(): return lax.psum(values, 'col')  215 us
  transfers between devices with their start and end apart: 10, of which 10 were waited for; matrix products, arithmetic and copies ran while one was open for 1% of the time, Pallas kernels for 0%

commit v1 on v0

--- a/solution.py
+++ b/solution.py
@@ -5,7 +5,7 @@
 
 
 def col_sum(values):
-    return lax.psum(values, "col")
+    return jnp.sum(lax.all_gather(values, "col"), axis=0)
 
 
 def row_sum(values):

time: 1500 us -> 1330 us (0.89)
  waiting for transfers between devices: 1440 us -> 1230 us
  blocking collectives: 0 us -> 33.8 us
    psum x5 -> x0, waiting for transfers between devices: 215 us -> none  [col_sum(): return lax.psum(values, 'col')]
    all_gather x0 -> x4, blocking collectives: none -> 33.8 us  [col_sum(): return jnp.sum(lax.all_gather(values, 'col'), axis=0)]
    all_gather x0 -> x1, waiting for transfers between devices: none -> 21.3 us  [col_sum(): return jnp.sum(lax.all_gather(values, 'col'), axis=0)]
  transfers between devices with their start and end apart: 10 -> 6, of which waited for: 10 -> 6; matrix products, arithmetic and copies ran while one was open for 1% -> 1% of each run, Pallas kernels for 0% -> 0%
where the time goes in v1:
time: 1330 us
  waiting for transfers between devices  1230 us (92%)
  blocking collectives  33.8 us (3%)
  matrix products  33.2 us (2%)
  local copies, waits for them, and re-layouts  15.7 us (1%)
  between operations  14.2 us (1%)
    psum x1, waiting for transfers between devices, root_total(): return lax.psum(values, ('layer', 'row'))  609 us
    psum x4, waiting for transfers between devices, row_sum(): return lax.psum(values, 'row')  596 us
    all_gather x4, blocking collectives, col_sum(): return jnp.sum(lax.all_gather(values, 'col'), axis=0)  33.8 us
  transfers between devices with their start and end apart: 6, of which 6 were waited for; matrix products, arithmetic and copies ran while one was open for 1% of the time, Pallas kernels for 0%

profile of v1, /device:TPU:2, one launch (start us, length us, event | category | flops | bytes accessed | tf_op | source)
XLA Modules:
  0.0 1330.6 jit_solution(14329407301621851748)
XLA Ops:
  7.2 1.9 fusion.18
  9.1 8.7 all-gather
  17.8 1.1 reduce_sum.45
  18.9 1.4 convolution_bitcast_fusion.2
  20.4 3.7 convolution_bitcast_fusion
  24.1 149.9 %all-reduce.6.cloned.1.call-done = f32[2048,128]{1,0:T(8,128)} async-done(((f32[2048,128]{1,0:T(8,128)}), f32[2048,128]{1,0:T(8,128)}) %all-reduce.6.cloned.1.call-update) | async-done | bytes 1048592 | tf_op jit(solution)/shard_map/psum | solution.py:12
  174.0 2.0 convolution_bitcast_fusion.6
  176.0 8.5 all-gather.1
  184.5 2.1 reshape.9
  186.6 1.4 reduce_sum.46
  187.9 3.7 fusion
  191.7 609.5 %all-reduce.8.cloned.1.call-done = f32[4096,128]{1,0:T(8,128)} async-done(((f32[4096,128]{1,0:T(8,128)}), f32[4096,128]{1,0:T(8,128)}) %all-reduce.8.cloned.1.call-update) | async-done | bytes 2097168 | tf_op jit(solution)/shard_map/psum | solution.py:16
  801.2 5.7 convolution_bitcast_fusion.5
  806.9 21.3 %all-gather.7.cloned.1.call-done = f32[2048,128]{0,1:T(8,128)} async-done(((f32[512,128]{0,1:T(8,128)}), f32[2048,128]{0,1:T(8,128)}) %all-gather.7.cloned.1.call-update) | async-done | bytes 1048592 | tf_op jit(solution)/shard_map/all_gather | solution.py:8
  828.2 2.9 reshape.10
  831.1 1.8 reduce_sum.47
  833.0 4.2 convolution_bitcast_fusion.1
  837.3 154.9 %all-reduce.10.cloned.1.call-done = f32[4096,128]{0,1:T(8,128)} async-done(((f32[4096,128]{0,1:T(8,128)}), f32[4096,128]{0,1:T(8,128)}) %all-reduce.10.cloned.1.call-update) | async-done | bytes 2097168 | tf_op jit(solution)/shard_map/psum | solution.py:12
  992.2 2.0 fusion.4
  994.3 8.5 all-gather.3
  1002.7 2.1 reshape.11
  1004.8 2.0 reduce_sum.48
  1006.8 2.2 convolution_bitcast_fusion.3
  1009.1 148.0 %all-reduce.12.cloned.1.call-done = f32[2048,128]{0,1:T(8,128)} async-done(((f32[2048,128]{0,1:T(8,128)}), f32[2048,128]{0,1:T(8,128)}) %all-reduce.12.cloned.1.call-update) | async-done | bytes 1048592 | tf_op jit(solution)/shard_map/psum | solution.py:12
  1157.1 2.0 fusion.13
  1159.3 2.1 fusion.7
  1162.2 8.2 all-gather.4
  1171.1 2.2 convolution_bitcast_fusion.4
  1174.2 3.0 copy.18
  1177.1 1.3 copy.19
  1178.4 142.7 %all-reduce.14.cloned.1.call-done = f32[2,1024,128]{1,2,0:T(8,128)} async-done(((f32[2,1024,128]{1,2,0:T(8,128)}), f32[2,1024,128]{1,2,0:T(8,128)}) %all-reduce.14.cloned.1.call-update) | async-done | bytes 1048592 | tf_op jit(solution)/shard_map/psum | solution.py:12
  1321.2 2.5 copy.20
  (29 shorter events, 2.9 us)
Async XLA Ops:
  7.2 180.8 %copy-start = (bf16[1,4096,256]{2,1,0:T(8,128)(2,1)S(1)}, bf16[1,4096,256]{2,1,0:T(8,128)(2,1)}, u32[]{:S(2)}) copy-start(bf16[1,4096,256]{2,1,0:T(8,128)(2,1)} %param.17) | copy-start | bytes 6291460
  7.2 11.7 copy-start.3
  7.2 166.8 %all-reduce.6.cloned.1.call-start = ((), (), s32[]{:S(2)}) async-start(), calls=%async_computation | async-start | bytes 2097152 | tf_op jit(solution)/shard_map/psum | solution.py:12
  20.3 153.7 %copy-start.2 = (bf16[1,256,2048]{2,1,0:T(8,128)(2,1)S(1)}, bf16[1,256,2048]{2,1,0:T(8,128)(2,1)}, u32[]{:S(2)}) copy-start(bf16[1,256,2048]{2,1,0:T(8,128)(2,1)} %param.13) | copy-start | bytes 3145732
  20.4 780.8 %all-reduce.8.cloned.1.call-start = ((), (), s32[]{:S(2)}) async-start(), calls=%async_computation.1 | async-start | bytes 4194304 | tf_op jit(solution)/shard_map/psum | solution.py:16
  187.9 3.7 copy-start.6
  191.6 636.6 %all-gather.7.cloned.1.call-start = ((), (), s32[]{:S(2)}) async-start(), calls=%async_computation.5 | async-start | bytes 1310720 | tf_op jit(solution)/shard_map/all_gather | solution.py:8
  806.9 185.3 %all-reduce.10.cloned.1.call-start = ((), (), s32[]{:S(2)}) async-start(), calls=%async_computation.2 | async-start | bytes 4194304 | tf_op jit(solution)/shard_map/psum | solution.py:12
  837.2 319.9 %all-reduce.12.cloned.1.call-start = ((), (), s32[]{:S(2)}) async-start(), calls=%async_computation.3 | async-start | bytes 2097152 | tf_op jit(solution)/shard_map/psum | solution.py:12
  1009.1 312.1 %all-reduce.14.cloned.1.call-start = ((), (), s32[]{:S(2)}) async-start(), calls=%async_computation.4 | async-start | bytes 2097152 | tf_op jit(solution)/shard_map/psum | solution.py:12
  1157.1 2.2 copy-start.1
  1159.3 11.7 copy-start.5
  1174.2 3.0 copy-start.4
Sparse Core Ops, SparseCore 0:
  20.5 153.4 all-reduce.5
  191.8 609.3 all-reduce.7
  807.0 21.1 all-gather.6
  837.3 154.8 all-reduce.9
  1009.2 147.8 all-reduce.11
  1173.5 147.6 all-reduce.13
